TPU v7x, 32 devices: a whole 2x2x4 slice. The times are simulated.
32 devices in a mesh: shot: 4 (over z), sub: 8 (over y, x, core).
Axes of the slice: x: 2, y: 2, z: 4, core: 2. Of those that a mesh axis runs over, the one named last changes fastest.
Arguments:
- electric: float32 [4, 3, 32, 32, 128], P('shot', None, 'sub'), may hold values from -6 to 6
- magnetic: float32 [4, 3, 32, 32, 128], P('shot', None, 'sub'), may hold values from -6 to 6
- polar: float32 [4, 3, 32, 32, 128], P('shot', None, 'sub'), may hold values from -4 to 4
- adj_electric: float32 [4, 3, 32, 32, 128], P('shot', None, 'sub'), may hold values from -6 to 6
- adj_magnetic: float32 [4, 3, 32, 32, 128], P('shot', None, 'sub'), may hold values from -6 to 6
- adj_polar: float32 [4, 3, 32, 32, 128], P('shot', None, 'sub'), may hold values from -4 to 4
- permittivity: float32 [32, 32, 128], P('sub'), may hold values from 3 to 25
- conductivity: float32 [32, 32, 128], P('sub'), may hold values from 0.02 to 2
- debye_class: int32 [32, 32, 128], P('sub'), may hold values from 0 to 7
- debye_rate: float32 [8], replicated, may hold values from 0.3 to 0.95
- debye_strength: float32 [8], replicated, may hold values from 0.3 to 3
- wavelet: float32 [6], replicated, may hold values from -4 to 4
- src_cell: int32 [4, 64], P('shot'), may hold values from 0 to 131071
- src_sign: int32 [4, 64], P('shot'), may hold values from 0 to 1
- rec_owner: int32 [4, 1024, 1], P('shot', 'sub'), may hold values from 0 to 7; in each aligned block of 128 rows (0 to 127, 128 to 255, ..., all dimensions but the last counted through in order) at most 16 rows name the same one
- rec_pos: int32 [4, 1024], P('shot', 'sub'), may hold values from 0 to 16383
- observed: float32 [4, 6, 1024], P('shot', None, 'sub'), may hold values from -6 to 6
Outputs:
- grad_eps: float32 [32, 32, 128], P('sub')
- grad_sigma: float32 [32, 32, 128], P('sub')
Inputs may be any that keep to these rules, and one draw needn't show every extreme that they name: Receiver r of a shot group lies in the x range of slab rec_owner; among the 128 receivers of each aligned block of the list at most 16 have the same owner.
All inputs are finite; a program needn't handle non-finite values.
Results may differ from a plain program's by a relative error of at most 0.0001.
Values sent between devices are 32-bit elements; how exact they have to be, the bound alone decides.
No kernel may reach another device: no remote copies, remote signals or barrier semaphores. Data moves between devices by JAX's collectives and lax.ppermute only.
A program may use at most 64 MiB of HBM per device.

v0:
```python
import jax
import jax.numpy as jnp
from jax import lax
from jax.sharding import PartitionSpec as P

CAP = 16


def from_behind(block, axis, distance):
    devices = range(lax.axis_size(axis))
    route = [(i - distance, i) for i in devices if i - distance in devices]
    return lax.ppermute(block, axis, route)


def diff_forward(u, axis):
    tail = lax.slice_in_dim(u, 1, u.shape[axis], axis=axis)
    edge = jnp.zeros_like(lax.slice_in_dim(u, 0, 1, axis=axis))
    return jnp.concatenate([tail, edge], axis) - u


def diff_backward(u, axis):
    head = lax.slice_in_dim(u, 0, u.shape[axis] - 1, axis=axis)
    edge = jnp.zeros_like(lax.slice_in_dim(u, 0, 1, axis=axis))
    return u - jnp.concatenate([edge, head], axis)


def forward_across(u, plane):
    return jnp.concatenate([u[1:], plane], 0) - u


def backward_across(u, plane):
    return u - jnp.concatenate([plane, u[:-1]], 0)


def advance(state, coefs, inject):
    e_field, h_field, p_field = state
    coef_a, coef_b, rate, strength = coefs
    east = from_behind(e_field[1:3, 0:1], "sub", -1)
    curl_e = jnp.stack(
        [
            diff_forward(e_field[2], 2) - diff_forward(e_field[1], 1),
            diff_forward(e_field[0], 1) - forward_across(e_field[2], east[1]),
            forward_across(e_field[1], east[0]) - diff_forward(e_field[0], 2),
        ]
    )
    h_new = h_field - 0.5 * curl_e
    west = from_behind(h_new[1:3, -1:], "sub", 1)
    curl_h = jnp.stack(
        [
            diff_backward(h_new[2], 2) - diff_backward(h_new[1], 1),
            diff_backward(h_new[0], 1) - backward_across(h_new[2], west[1]),
            backward_across(h_new[1], west[0]) - diff_backward(h_new[0], 2),
        ]
    )
    e_new = coef_a * e_field + coef_b * (curl_h - p_field)
    e_new = e_new.at[1].add(inject)
    p_new = rate * p_field + (1.0 - rate) * strength * e_new
    return (e_new, h_new, p_new)


def lookup(table, classes):
    picks = classes[None] == jnp.arange(table.shape[0], dtype=jnp.int32)[:, None, None, None]
    return jnp.sum(jnp.where(picks, table[:, None, None, None], 0.0), axis=0)


def per_device(
    electric,
    magnetic,
    polar,
    adj_electric,
    adj_magnetic,
    adj_polar,
    permittivity,
    conductivity,
    debye_class,
    debye_rate,
    debye_strength,
    wavelet,
    src_cell,
    src_sign,
    rec_owner,
    rec_pos,
    observed,
):
    width, depth, span = permittivity.shape
    steps = wavelet.shape[0]
    nsub = lax.axis_size("sub")
    nshot = lax.axis_size("shot")
    mine = lax.axis_index("sub")
    ratio = conductivity / (2.0 * permittivity)
    coefs = (
        (1.0 - ratio) / (1.0 + ratio),
        0.5 / (permittivity * (1.0 + ratio)),
        lookup(debye_rate, debye_class),
        lookup(debye_strength, debye_class),
    )
    full_x = width * nsub
    flat = src_cell[0]
    src_global = flat % full_x
    src_y = flat // full_x % span
    src_z = flat // (full_x * span)
    src_local = src_global - mine * width
    src_live = (src_local >= 0) & (src_local < width)
    src_x = jnp.clip(src_local, 0, width - 1)
    src_amp = jnp.where(src_live, (2 * src_sign[0] - 1).astype(jnp.float32), 0.0)
    owners = rec_owner[0, :, 0]
    cellpos = rec_pos[0]
    traces = observed[0]
    hits = (owners[:, None] == jnp.arange(nsub, dtype=jnp.int32)[None, :]).astype(jnp.int32)
    before = jnp.cumsum(hits, axis=0) - hits
    slots = jnp.sum(hits * before, axis=1)
    target = owners * CAP + slots
    send_trace = jnp.zeros((steps, nsub * CAP), jnp.float32).at[:, target].set(traces)
    send_pos = jnp.full((1, nsub * CAP), -1, jnp.int32).at[0, target].set(cellpos)
    got_trace, got_pos = (
        lax.all_to_all(send_trace, "sub", split_axis=1, concat_axis=1, tiled=True),
        lax.all_to_all(send_pos, "sub", split_axis=1, concat_axis=1, tiled=True),
    )
    positions = got_pos[0]
    live = positions >= 0
    positions = jnp.where(live, positions, 0)
    rec_x = positions % width
    rec_y = positions // width % span
    rec_z = positions // (width * span)
    state = (electric[0], magnetic[0], polar[0])
    history = [electric[0]]
    synth = []
    for step in range(steps):
        source = (
            jnp.zeros((width, depth, span), jnp.float32)
            .at[src_x, src_z, src_y]
            .add(src_amp * wavelet[step])
        )
        state = advance(state, coefs, source)
        history.append(state[0])
        synth.append(state[0][1][rec_x, rec_z, rec_y])
    resid = jnp.where(live[None], jnp.stack(synth) - got_trace, 0.0)
    state = (adj_electric[0], adj_magnetic[0], adj_polar[0])
    corr_eps = jnp.zeros((width, depth, span), jnp.float32)
    corr_sigma = jnp.zeros((width, depth, span), jnp.float32)
    for back in range(steps):
        later = steps - back
        source = (
            jnp.zeros((width, depth, span), jnp.float32)
            .at[rec_x, rec_z, rec_y]
            .add(resid[later - 1])
        )
        state = advance(state, coefs, source)
        adjoint = state[0]
        term_eps = jnp.sum(adjoint * (history[later] - history[later - 1]), axis=0)
        term_sigma = jnp.sum(adjoint * history[later], axis=0)
        corr_eps = corr_eps + term_eps
        corr_sigma = corr_sigma + term_sigma
    corr_eps, corr_sigma = lax.psum((corr_eps, corr_sigma), "shot")
    return (-(corr_eps / (steps * nshot)), -(corr_sigma / (steps * nshot)))


def solution(mesh):
    in_specs = (
        P("shot", None, "sub", None, None),
        P("shot", None, "sub", None, None),
        P("shot", None, "sub", None, None),
        P("shot", None, "sub", None, None),
        P("shot", None, "sub", None, None),
        P("shot", None, "sub", None, None),
        P("sub", None, None),
        P("sub", None, None),
        P("sub", None, None),
        P(),
        P(),
        P(),
        P("shot", None),
        P("shot", None),
        P("shot", "sub", None),
        P("shot", "sub"),
        P("shot", None, "sub"),
    )
    out_specs = (P("sub", None, None), P("sub", None, None))
    return jax.shard_map(
        per_device, mesh=mesh, in_specs=in_specs, out_specs=out_specs, check_vma=False
    )
```

profile of v0, /device:TPU:0, one launch (start us, length us, event | category | flops | bytes accessed | tf_op | source)
XLA Modules:
  0.0 288.4 jit_solution(6837316200168095393)
XLA Ops:
  13.6 7.1 %all-to-all-start = ((s32[1,8,16]{2,0,1:T(1,128)}), s32[1,8,16]{2,0,1:T(1,128)S(1)}, u32[]{:S(2)}, u32[]{:S(2)}) async-start(s32[1,8,16]{2,0,1:T(1,128)} %bitcast.28), calls=%async_computation | async-start | bytes 8192 | tf_op jit(solution)/shard_map/all_to_all | solution.py:117
  28.0 3.2 %broadcast_multiply_fusion.1 = (f32[64]{0:T(128)S(1)}, f32[64]{0:T(128)S(1)}, f32[64]{0:T(128)S(1)}, f32[64]{0:T(128)S(1)}, f32[64]{0:T(128)S(1)}) fusion(f32[64]{0:T(128)S(1)} %get-tuple-element.205, f32[]{:T(128)} %bitcast.150, f32[]{:T(128)} %bitcast.127, f32[]{:T(128)} %bitcast.104, f32[]{:T(128)} %bitcast.81, f32[]{:T(128)} %bitcast.57), kind=kLoop, calls=%fused_computation.540 | loop fusion | flops 320 | bytes 1556 | tf_op jit(solution)/shard_map/mul | solution.py:132
  31.2 4.5 %scatter_fusion = f32[4,32,128]{2,1,0:T(8,128)S(1)} fusion(f32[4,32,128]{2,1,0:T(8,128)S(1)} %broadcast.880.clone, s32[64]{0:T(128)S(1)} %fusion.152, f32[64]{0:T(128)S(1)} %get-tuple-element.440), kind=kCustom, calls=%fused_computation.7 | custom fusion | flops 64 | bytes 1536 | tf_op jit(solution)/shard_map/scatter-add | solution.py:132
  35.7 4.5 %scatter_fusion.1 = f32[4,32,128]{2,1,0:T(8,128)S(1)} fusion(f32[4,32,128]{2,1,0:T(8,128)S(1)} %broadcast.880.clone.1, s32[64]{0:T(128)S(1)} %fusion.152, f32[64]{0:T(128)S(1)} %get-tuple-element.439), kind=kCustom, calls=%fused_computation.8 | custom fusion | flops 64 | bytes 1536 | tf_op jit(solution)/shard_map/scatter-add | solution.py:132
  40.2 4.5 %scatter_fusion.2 = f32[4,32,128]{2,1,0:T(8,128)S(1)} fusion(f32[4,32,128]{2,1,0:T(8,128)S(1)} %broadcast.880.clone.2, s32[64]{0:T(128)S(1)} %fusion.152, f32[64]{0:T(128)S(1)} %get-tuple-element.438), kind=kCustom, calls=%fused_computation.9 | custom fusion | flops 64 | bytes 1536 | tf_op jit(solution)/shard_map/scatter-add | solution.py:132
  44.7 4.5 %scatter_fusion.3 = f32[4,32,128]{2,1,0:T(8,128)S(1)} fusion(f32[4,32,128]{2,1,0:T(8,128)S(1)} %broadcast.880.clone.3, s32[64]{0:T(128)S(1)} %fusion.152, f32[64]{0:T(128)S(1)} %get-tuple-element.437), kind=kCustom, calls=%fused_computation.10 | custom fusion | flops 64 | bytes 1536 | tf_op jit(solution)/shard_map/scatter-add | solution.py:132
  49.2 4.5 %scatter_fusion.4 = f32[4,32,128]{2,1,0:T(8,128)S(1)} fusion(f32[4,32,128]{2,1,0:T(8,128)S(1)} %broadcast.880.clone.4, s32[64]{0:T(128)S(1)} %fusion.152, f32[64]{0:T(128)S(1)} %get-tuple-element.436), kind=kCustom, calls=%fused_computation.11 | custom fusion | flops 64 | bytes 1536 | tf_op jit(solution)/shard_map/scatter-add | solution.py:132
  53.7 4.5 %scatter_fusion.5 = f32[4,32,128]{2,1,0:T(8,128)S(1)} fusion(f32[4,32,128]{2,1,0:T(8,128)S(1)} %broadcast.880.clone.6, s32[64]{0:T(128)S(1)} %fusion.152, f32[64]{0:T(128)S(1)} %get-tuple-element.204), kind=kCustom, calls=%fused_computation.12 | custom fusion | flops 64 | bytes 1536 | tf_op jit(solution)/shard_map/scatter-add | solution.py:132
  58.2 4.1 %all-to-all-start.1 = ((f32[6,8,16]{2,0,1:T(8,128)}), f32[6,8,16]{2,0,1:T(8,128)S(1)}, u32[]{:S(2)}, u32[]{:S(2)}) async-start(f32[6,8,16]{2,0,1:T(8,128)} %copy.45), calls=%async_computation.1 | async-start | bytes 65536 | tf_op jit(solution)/shard_map/all_to_all | solution.py:116
  64.3 2.9 %all-to-all-done.1 = f32[6,8,16]{2,0,1:T(8,128)S(1)} async-done(((f32[6,8,16]{2,0,1:T(8,128)}), f32[6,8,16]{2,0,1:T(8,128)S(1)}, u32[]{:S(2)}, u32[]{:S(2)}) %all-to-all-start.1) | async-done | bytes 3104 | tf_op jit(solution)/shard_map/all_to_all | solution.py:116
  71.6 2.9 collective-permute-start.1
  79.5 3.4 %collective-permute-start.5 = (f32[2,1,32,128]{3,2,1,0:T(8,128)S(1)}, f32[2,1,32,128]{3,2,1,0:T(8,128)S(1)}, u32[]{:S(2)}, u32[]{:S(2)}) collective-permute-start(f32[2,1,32,128]{3,2,1,0:T(8,128)S(1)} %slice.1953), channel_id=1, source_target_pairs={{0,1},{1,2},{2,3},{3,4},{4,5},{5,6},{6,7},{8,9},{9,10},{10,11},{11... | collective-permute-start | bytes 98312 | tf_op jit(solution)/shard_map/ppermute | solution.py:12
  87.9 5.1 %collective-permute-start.7 = (f32[2,1,32,128]{3,2,1,0:T(8,128)S(1)}, f32[2,1,32,128]{3,2,1,0:T(8,128)S(1)}, u32[]{:S(2)}, u32[]{:S(2)}) collective-permute-start(f32[2,1,32,128]{3,2,1,0:T(8,128)S(1)} %slice.1977), channel_id=1, source_target_pairs={{0,1},{1,2},{2,3},{3,4},{4,5},{5,6},{6,7},{8,9},{9,10},{10,11},{11... | collective-permute-start | bytes 98312 | tf_op jit(solution)/shard_map/ppermute | solution.py:12
  98.6 5.0 %collective-permute-start.9 = (f32[2,1,32,128]{3,2,1,0:T(8,128)S(1)}, f32[2,1,32,128]{3,2,1,0:T(8,128)S(1)}, u32[]{:S(2)}, u32[]{:S(2)}) collective-permute-start(f32[2,1,32,128]{3,2,1,0:T(8,128)S(1)} %slice.2001), channel_id=1, source_target_pairs={{0,1},{1,2},{2,3},{3,4},{4,5},{5,6},{6,7},{8,9},{9,10},{10,11},{11... | collective-permute-start | bytes 98312 | tf_op jit(solution)/shard_map/ppermute | solution.py:12
  108.1 2.0 gather_fusion.3
  112.1 3.6 %collective-permute-start.11 = (f32[2,1,32,128]{3,2,1,0:T(8,128)S(1)}, f32[2,1,32,128]{3,2,1,0:T(8,128)S(1)}, u32[]{:S(2)}, u32[]{:S(2)}) collective-permute-start(f32[2,1,32,128]{3,2,1,0:T(8,128)S(1)} %slice.2025), channel_id=1, source_target_pairs={{0,1},{1,2},{2,3},{3,4},{4,5},{5,6},{6,7},{8,9},{9,10},{10,11},{11... | collective-permute-start | bytes 98312 | tf_op jit(solution)/shard_map/ppermute | solution.py:12
  121.2 2.1 gather_fusion.4
  126.0 5.1 %collective-permute-start.13 = (f32[2,1,32,128]{3,2,1,0:T(8,128)S(1)}, f32[2,1,32,128]{3,2,1,0:T(8,128)S(1)}, u32[]{:S(2)}, u32[]{:S(2)}) collective-permute-start(f32[2,1,32,128]{3,2,1,0:T(8,128)S(1)} %slice.2049), channel_id=1, source_target_pairs={{0,1},{1,2},{2,3},{3,4},{4,5},{5,6},{6,7},{8,9},{9,10},{10,11},{11... | collective-permute-start | bytes 98312 | tf_op jit(solution)/shard_map/ppermute | solution.py:12
  135.9 8.3 %scatter_fusion.6 = f32[4,32,128]{2,1,0:T(8,128)S(1)} fusion(f32[4,32,128]{2,1,0:T(8,128)S(1)} %broadcast.880.clone.5, s32[128]{0:T(128)S(1)} %get-tuple-element.216, f32[128]{0:T(128)S(1)} %get-tuple-element.185), kind=kCustom, calls=%fused_computation.14 | custom fusion | flops 128 | bytes 3072 | tf_op jit(solution)/shard_map/scatter-add | solution.py:146
  145.9 8.3 %scatter_fusion.7 = f32[4,32,128]{2,1,0:T(8,128)S(1)} fusion(f32[4,32,128]{2,1,0:T(8,128)S(1)} %broadcast.880.clone.7, s32[128]{0:T(128)S(1)} %get-tuple-element.216, f32[128]{0:T(128)S(1)} %get-tuple-element.184), kind=kCustom, calls=%fused_computation.15 | custom fusion | flops 128 | bytes 3072 | tf_op jit(solution)/shard_map/scatter-add | solution.py:146
  154.2 8.3 %scatter_fusion.8 = f32[4,32,128]{2,1,0:T(8,128)S(1)} fusion(f32[4,32,128]{2,1,0:T(8,128)S(1)} %broadcast.880.clone.8, s32[128]{0:T(128)S(1)} %get-tuple-element.216, f32[128]{0:T(128)S(1)} %get-tuple-element.183), kind=kCustom, calls=%fused_computation.16 | custom fusion | flops 128 | bytes 3072 | tf_op jit(solution)/shard_map/scatter-add | solution.py:146
  162.5 8.3 %scatter_fusion.9 = f32[4,32,128]{2,1,0:T(8,128)S(1)} fusion(f32[4,32,128]{2,1,0:T(8,128)S(1)} %broadcast.880.clone.9, s32[128]{0:T(128)S(1)} %get-tuple-element.216, f32[128]{0:T(128)S(1)} %get-tuple-element.182), kind=kCustom, calls=%fused_computation.17 | custom fusion | flops 128 | bytes 3072 | tf_op jit(solution)/shard_map/scatter-add | solution.py:146
  170.9 8.3 %scatter_fusion.10 = f32[4,32,128]{2,1,0:T(8,128)S(1)} fusion(f32[4,32,128]{2,1,0:T(8,128)S(1)} %broadcast.880.clone.10, s32[128]{0:T(128)S(1)} %get-tuple-element.216, f32[128]{0:T(128)S(1)} %get-tuple-element.181), kind=kCustom, calls=%fused_computation.18 | custom fusion | flops 128 | bytes 3072 | tf_op jit(solution)/shard_map/scatter-add | solution.py:146
  179.2 8.3 %scatter_fusion.11 = f32[4,32,128]{2,1,0:T(8,128)S(1)} fusion(f32[4,32,128]{2,1,0:T(8,128)S(1)} %broadcast.880.clone.11, s32[128]{0:T(128)S(1)} %get-tuple-element.216, f32[128]{0:T(128)S(1)} %get-tuple-element.180), kind=kCustom, calls=%fused_computation.19 | custom fusion | flops 128 | bytes 3072 | tf_op jit(solution)/shard_map/scatter-add | solution.py:146
  187.7 4.4 %collective-permute-start.15 = (f32[2,1,32,128]{3,2,1,0:T(8,128)S(1)}, f32[2,1,32,128]{3,2,1,0:T(8,128)S(1)}, u32[]{:S(2)}, u32[]{:S(2)}) collective-permute-start(f32[2,1,32,128]{3,2,1,0:T(8,128)S(1)} %slice.2074), channel_id=1, source_target_pairs={{0,1},{1,2},{2,3},{3,4},{4,5},{5,6},{6,7},{8,9},{9,10},{10,11},{11... | collective-permute-start | bytes 98312 | tf_op jit(solution)/shard_map/ppermute | solution.py:12
  194.8 4.4 %collective-permute-done.16 = f32[2,1,32,128]{3,2,1,0:T(8,128)S(1)} collective-permute-done((f32[2,1,32,128]{3,2,1,0:T(8,128)S(1)}, f32[2,1,32,128]{3,2,1,0:T(8,128)S(1)}, u32[]{:S(2)}, u32[]{:S(2)}) %collective-permute-start.16) | collective-permute-done | bytes 32800 | tf_op jit(solution)/shard_map/ppermute | solution.py:12
  199.4 5.1 %collective-permute-start.17 = (f32[2,1,32,128]{3,2,1,0:T(8,128)S(1)}, f32[2,1,32,128]{3,2,1,0:T(8,128)S(1)}, u32[]{:S(2)}, u32[]{:S(2)}) collective-permute-start(f32[2,1,32,128]{3,2,1,0:T(8,128)S(1)} %slice.2099), channel_id=1, source_target_pairs={{0,1},{1,2},{2,3},{3,4},{4,5},{5,6},{6,7},{8,9},{9,10},{10,11},{11... | collective-permute-start | bytes 98312 | tf_op jit(solution)/shard_map/ppermute | solution.py:12
  207.2 3.4 %collective-permute-done.18 = f32[2,1,32,128]{3,2,1,0:T(8,128)S(1)} collective-permute-done((f32[2,1,32,128]{3,2,1,0:T(8,128)S(1)}, f32[2,1,32,128]{3,2,1,0:T(8,128)S(1)}, u32[]{:S(2)}, u32[]{:S(2)}) %collective-permute-start.18) | collective-permute-done | bytes 32800 | tf_op jit(solution)/shard_map/ppermute | solution.py:12
  210.7 6.7 %collective-permute-start.19 = (f32[2,1,32,128]{3,2,1,0:T(8,128)S(1)}, f32[2,1,32,128]{3,2,1,0:T(8,128)S(1)}, u32[]{:S(2)}, u32[]{:S(2)}) collective-permute-start(f32[2,1,32,128]{3,2,1,0:T(8,128)S(1)} %slice.2124), channel_id=1, source_target_pairs={{0,1},{1,2},{2,3},{3,4},{4,5},{5,6},{6,7},{8,9},{9,10},{10,11},{11... | collective-permute-start | bytes 98312 | tf_op jit(solution)/shard_map/ppermute | solution.py:12
  222.0 5.7 %collective-permute-start.21 = (f32[2,1,32,128]{3,2,1,0:T(8,128)S(1)}, f32[2,1,32,128]{3,2,1,0:T(8,128)S(1)}, u32[]{:S(2)}, u32[]{:S(2)}) collective-permute-start(f32[2,1,32,128]{3,2,1,0:T(8,128)S(1)} %slice.2149), channel_id=1, source_target_pairs={{0,1},{1,2},{2,3},{3,4},{4,5},{5,6},{6,7},{8,9},{9,10},{10,11},{11... | collective-permute-start | bytes 98312 | tf_op jit(solution)/shard_map/ppermute | solution.py:12
  232.2 5.7 %collective-permute-start.23 = (f32[2,1,32,128]{3,2,1,0:T(8,128)S(1)}, f32[2,1,32,128]{3,2,1,0:T(8,128)S(1)}, u32[]{:S(2)}, u32[]{:S(2)}) collective-permute-start(f32[2,1,32,128]{3,2,1,0:T(8,128)S(1)} %slice.2174), channel_id=1, source_target_pairs={{0,1},{1,2},{2,3},{3,4},{4,5},{5,6},{6,7},{8,9},{9,10},{10,11},{11... | collective-permute-start | bytes 98312 | tf_op jit(solution)/shard_map/ppermute | solution.py:12
  240.7 38.6 %all-reduce.100.cloned.1.call-done = (f32[4,32,128]{2,1,0:T(8,128)}, f32[4,32,128]{2,1,0:T(8,128)}) async-done(((f32[4,32,128]{2,1,0:T(8,128)}, f32[4,32,128]{2,1,0:T(8,128)}), (f32[4,32,128]{2,1,0:T(8,128)}, f32[4,32,128]{2,1,0:T(8,128)})) %all-reduce.100.cloned.1.call-update) | async-done | bytes 131088 | tf_op jit(solution)/shard_map/psum | solution.py:154
  (378 shorter events, 75.1 us)
Async XLA Ops:
  7.2 4.2 %copy-start.31 = (s32[1,128,1]{1,2,0:T(1,128)S(1)}, s32[1,128,1]{1,2,0:T(1,128)}, u32[]{:S(2)}) copy-start(s32[1,128,1]{1,2,0:T(1,128)} %param.55) | copy-start | bytes 1540
  7.2 13.5 %copy-start.2 = (f32[1,3,4,32,128]{4,3,2,1,0:T(8,128)S(1)}, f32[1,3,4,32,128]{4,3,2,1,0:T(8,128)}, u32[]{:S(2)}) copy-start(f32[1,3,4,32,128]{4,3,2,1,0:T(8,128)} %param.41) | copy-start | bytes 589828
  8.0 59.9 %collective-permute-start.2 = (f32[2,1,32,128]{3,2,1,0:T(8,128)S(1)}, f32[2,1,32,128]{3,2,1,0:T(8,128)S(1)}, u32[]{:S(2)}, u32[]{:S(2)}) collective-permute-start(f32[2,1,32,128]{3,2,1,0:T(8,128)S(1)} %slice.1919), channel_id=1, source_target_pairs={{1,0},{2,1},{3,2},{4,3},{5,4},{6,5},{7,6},{9,8},{10,9},{11,10},{12... | collective-permute-start | bytes 98312 | tf_op jit(solution)/shard_map/ppermute | solution.py:12
  10.1 60.5 %collective-permute-start = (f32[2,1,32,128]{3,2,1,0:T(8,128)S(1)}, f32[2,1,32,128]{3,2,1,0:T(8,128)S(1)}, u32[]{:S(2)}, u32[]{:S(2)}) collective-permute-start(f32[2,1,32,128]{3,2,1,0:T(8,128)S(1)} %slice.1899), channel_id=1, source_target_pairs={{1,0},{2,1},{3,2},{4,3},{5,4},{6,5},{7,6},{9,8},{10,9},{11,10},{12... | collective-permute-start | bytes 98312 | tf_op jit(solution)/shard_map/ppermute | solution.py:12
  13.6 44.6 %all-to-all-start = ((s32[1,8,16]{2,0,1:T(1,128)}), s32[1,8,16]{2,0,1:T(1,128)S(1)}, u32[]{:S(2)}, u32[]{:S(2)}) async-start(s32[1,8,16]{2,0,1:T(1,128)} %bitcast.28), calls=%async_computation | async-start | bytes 8192 | tf_op jit(solution)/shard_map/all_to_all | solution.py:117
  24.0 1.7 copy-start.28
  25.7 2.0 copy-start.25
  58.2 8.9 %all-to-all-start.1 = ((f32[6,8,16]{2,0,1:T(8,128)}), f32[6,8,16]{2,0,1:T(8,128)S(1)}, u32[]{:S(2)}, u32[]{:S(2)}) async-start(f32[6,8,16]{2,0,1:T(8,128)} %copy.45), calls=%async_computation.1 | async-start | bytes 65536 | tf_op jit(solution)/shard_map/all_to_all | solution.py:116
  62.3 217.0 %all-reduce.100.cloned.1.call-start = ((), (), s32[]{:S(2)}) async-start(), calls=%async_computation.2 | async-start | bytes 262144 | tf_op jit(solution)/shard_map/psum | solution.py:154
  68.9 5.5 %collective-permute-start.3 = (f32[2,1,32,128]{3,2,1,0:T(8,128)S(1)}, f32[2,1,32,128]{3,2,1,0:T(8,128)S(1)}, u32[]{:S(2)}, u32[]{:S(2)}) collective-permute-start(f32[2,1,32,128]{3,2,1,0:T(8,128)S(1)} %slice.1929), channel_id=1, source_target_pairs={{0,1},{1,2},{2,3},{3,4},{4,5},{5,6},{6,7},{8,9},{9,10},{10,11},{11... | collective-permute-start | bytes 98312 | tf_op jit(solution)/shard_map/ppermute | solution.py:12
  71.6 5.2 %collective-permute-start.1 = (f32[2,1,32,128]{3,2,1,0:T(8,128)S(1)}, f32[2,1,32,128]{3,2,1,0:T(8,128)S(1)}, u32[]{:S(2)}, u32[]{:S(2)}) collective-permute-start(f32[2,1,32,128]{3,2,1,0:T(8,128)S(1)} %slice.1909), channel_id=1, source_target_pairs={{0,1},{1,2},{2,3},{3,4},{4,5},{5,6},{6,7},{8,9},{9,10},{10,11},{11... | collective-permute-start | bytes 98312 | tf_op jit(solution)/shard_map/ppermute | solution.py:12
  75.6 3.8 %collective-permute-start.4 = (f32[2,1,32,128]{3,2,1,0:T(8,128)S(1)}, f32[2,1,32,128]{3,2,1,0:T(8,128)S(1)}, u32[]{:S(2)}, u32[]{:S(2)}) collective-permute-start(f32[2,1,32,128]{3,2,1,0:T(8,128)S(1)} %slice.1942), channel_id=1, source_target_pairs={{1,0},{2,1},{3,2},{4,3},{5,4},{6,5},{7,6},{9,8},{10,9},{11,10},{12... | collective-permute-start | bytes 98312 | tf_op jit(solution)/shard_map/ppermute | solution.py:12
  79.5 4.2 %collective-permute-start.5 = (f32[2,1,32,128]{3,2,1,0:T(8,128)S(1)}, f32[2,1,32,128]{3,2,1,0:T(8,128)S(1)}, u32[]{:S(2)}, u32[]{:S(2)}) collective-permute-start(f32[2,1,32,128]{3,2,1,0:T(8,128)S(1)} %slice.1953), channel_id=1, source_target_pairs={{0,1},{1,2},{2,3},{3,4},{4,5},{5,6},{6,7},{8,9},{9,10},{10,11},{11... | collective-permute-start | bytes 98312 | tf_op jit(solution)/shard_map/ppermute | solution.py:12
  84.0 3.7 %collective-permute-start.6 = (f32[2,1,32,128]{3,2,1,0:T(8,128)S(1)}, f32[2,1,32,128]{3,2,1,0:T(8,128)S(1)}, u32[]{:S(2)}, u32[]{:S(2)}) collective-permute-start(f32[2,1,32,128]{3,2,1,0:T(8,128)S(1)} %slice.1966), channel_id=1, source_target_pairs={{1,0},{2,1},{3,2},{4,3},{5,4},{6,5},{7,6},{9,8},{10,9},{11,10},{12... | collective-permute-start | bytes 98312 | tf_op jit(solution)/shard_map/ppermute | solution.py:12
  87.9 6.0 %collective-permute-start.7 = (f32[2,1,32,128]{3,2,1,0:T(8,128)S(1)}, f32[2,1,32,128]{3,2,1,0:T(8,128)S(1)}, u32[]{:S(2)}, u32[]{:S(2)}) collective-permute-start(f32[2,1,32,128]{3,2,1,0:T(8,128)S(1)} %slice.1977), channel_id=1, source_target_pairs={{0,1},{1,2},{2,3},{3,4},{4,5},{5,6},{6,7},{8,9},{9,10},{10,11},{11... | collective-permute-start | bytes 98312 | tf_op jit(solution)/shard_map/ppermute | solution.py:12
  94.2 3.7 %collective-permute-start.8 = (f32[2,1,32,128]{3,2,1,0:T(8,128)S(1)}, f32[2,1,32,128]{3,2,1,0:T(8,128)S(1)}, u32[]{:S(2)}, u32[]{:S(2)}) collective-permute-start(f32[2,1,32,128]{3,2,1,0:T(8,128)S(1)} %slice.1990), channel_id=1, source_target_pairs={{1,0},{2,1},{3,2},{4,3},{5,4},{6,5},{7,6},{9,8},{10,9},{11,10},{12... | collective-permute-start | bytes 98312 | tf_op jit(solution)/shard_map/ppermute | solution.py:12
  98.6 5.9 %collective-permute-start.9 = (f32[2,1,32,128]{3,2,1,0:T(8,128)S(1)}, f32[2,1,32,128]{3,2,1,0:T(8,128)S(1)}, u32[]{:S(2)}, u32[]{:S(2)}) collective-permute-start(f32[2,1,32,128]{3,2,1,0:T(8,128)S(1)} %slice.2001), channel_id=1, source_target_pairs={{0,1},{1,2},{2,3},{3,4},{4,5},{5,6},{6,7},{8,9},{9,10},{10,11},{11... | collective-permute-start | bytes 98312 | tf_op jit(solution)/shard_map/ppermute | solution.py:12
  105.4 4.8 %collective-permute-start.10 = (f32[2,1,32,128]{3,2,1,0:T(8,128)S(1)}, f32[2,1,32,128]{3,2,1,0:T(8,128)S(1)}, u32[]{:S(2)}, u32[]{:S(2)}) collective-permute-start(f32[2,1,32,128]{3,2,1,0:T(8,128)S(1)} %slice.2014), channel_id=1, source_target_pairs={{1,0},{2,1},{3,2},{4,3},{5,4},{6,5},{7,6},{9,8},{10,9},{11,10},{12... | collective-permute-start | bytes 98312 | tf_op jit(solution)/shard_map/ppermute | solution.py:12
  112.1 4.4 %collective-permute-start.11 = (f32[2,1,32,128]{3,2,1,0:T(8,128)S(1)}, f32[2,1,32,128]{3,2,1,0:T(8,128)S(1)}, u32[]{:S(2)}, u32[]{:S(2)}) collective-permute-start(f32[2,1,32,128]{3,2,1,0:T(8,128)S(1)} %slice.2025), channel_id=1, source_target_pairs={{0,1},{1,2},{2,3},{3,4},{4,5},{5,6},{6,7},{8,9},{9,10},{10,11},{11... | collective-permute-start | bytes 98312 | tf_op jit(solution)/shard_map/ppermute | solution.py:12
  118.6 5.6 %collective-permute-start.12 = (f32[2,1,32,128]{3,2,1,0:T(8,128)}, f32[2,1,32,128]{3,2,1,0:T(8,128)}, u32[]{:S(2)}, u32[]{:S(2)}) collective-permute-start(f32[2,1,32,128]{3,2,1,0:T(8,128)} %slice.2038), channel_id=1, source_target_pairs={{1,0},{2,1},{3,2},{4,3},{5,4},{6,5},{7,6},{9,8},{10,9},{11,10},{12... | collective-permute-start | bytes 98312 | tf_op jit(solution)/shard_map/ppermute | solution.py:12
  121.2 2.1 copy-start.20
  126.0 5.9 %collective-permute-start.13 = (f32[2,1,32,128]{3,2,1,0:T(8,128)S(1)}, f32[2,1,32,128]{3,2,1,0:T(8,128)S(1)}, u32[]{:S(2)}, u32[]{:S(2)}) collective-permute-start(f32[2,1,32,128]{3,2,1,0:T(8,128)S(1)} %slice.2049), channel_id=1, source_target_pairs={{0,1},{1,2},{2,3},{3,4},{4,5},{5,6},{6,7},{8,9},{9,10},{10,11},{11... | collective-permute-start | bytes 98312 | tf_op jit(solution)/shard_map/ppermute | solution.py:12
  144.3 43.2 %collective-permute-start.14 = (f32[2,1,32,128]{3,2,1,0:T(8,128)S(1)}, f32[2,1,32,128]{3,2,1,0:T(8,128)S(1)}, u32[]{:S(2)}, u32[]{:S(2)}) collective-permute-start(f32[2,1,32,128]{3,2,1,0:T(8,128)S(1)} %slice.2063), channel_id=1, source_target_pairs={{1,0},{2,1},{3,2},{4,3},{5,4},{6,5},{7,6},{9,8},{10,9},{11,10},{12... | collective-permute-start | bytes 98312 | tf_op jit(solution)/shard_map/ppermute | solution.py:12
  187.7 5.3 %collective-permute-start.15 = (f32[2,1,32,128]{3,2,1,0:T(8,128)S(1)}, f32[2,1,32,128]{3,2,1,0:T(8,128)S(1)}, u32[]{:S(2)}, u32[]{:S(2)}) collective-permute-start(f32[2,1,32,128]{3,2,1,0:T(8,128)S(1)} %slice.2074), channel_id=1, source_target_pairs={{0,1},{1,2},{2,3},{3,4},{4,5},{5,6},{6,7},{8,9},{9,10},{10,11},{11... | collective-permute-start | bytes 98312 | tf_op jit(solution)/shard_map/ppermute | solution.py:12
  193.3 5.9 %collective-permute-start.16 = (f32[2,1,32,128]{3,2,1,0:T(8,128)S(1)}, f32[2,1,32,128]{3,2,1,0:T(8,128)S(1)}, u32[]{:S(2)}, u32[]{:S(2)}) collective-permute-start(f32[2,1,32,128]{3,2,1,0:T(8,128)S(1)} %slice.2088), channel_id=1, source_target_pairs={{1,0},{2,1},{3,2},{4,3},{5,4},{6,5},{7,6},{9,8},{10,9},{11,10},{12... | collective-permute-start | bytes 98312 | tf_op jit(solution)/shard_map/ppermute | solution.py:12
  199.4 6.0 %collective-permute-start.17 = (f32[2,1,32,128]{3,2,1,0:T(8,128)S(1)}, f32[2,1,32,128]{3,2,1,0:T(8,128)S(1)}, u32[]{:S(2)}, u32[]{:S(2)}) collective-permute-start(f32[2,1,32,128]{3,2,1,0:T(8,128)S(1)} %slice.2099), channel_id=1, source_target_pairs={{0,1},{1,2},{2,3},{3,4},{4,5},{5,6},{6,7},{8,9},{9,10},{10,11},{11... | collective-permute-start | bytes 98312 | tf_op jit(solution)/shard_map/ppermute | solution.py:12
  205.7 4.9 %collective-permute-start.18 = (f32[2,1,32,128]{3,2,1,0:T(8,128)S(1)}, f32[2,1,32,128]{3,2,1,0:T(8,128)S(1)}, u32[]{:S(2)}, u32[]{:S(2)}) collective-permute-start(f32[2,1,32,128]{3,2,1,0:T(8,128)S(1)} %slice.2113), channel_id=1, source_target_pairs={{1,0},{2,1},{3,2},{4,3},{5,4},{6,5},{7,6},{9,8},{10,9},{11,10},{12... | collective-permute-start | bytes 98312 | tf_op jit(solution)/shard_map/ppermute | solution.py:12
  210.7 7.6 %collective-permute-start.19 = (f32[2,1,32,128]{3,2,1,0:T(8,128)S(1)}, f32[2,1,32,128]{3,2,1,0:T(8,128)S(1)}, u32[]{:S(2)}, u32[]{:S(2)}) collective-permute-start(f32[2,1,32,128]{3,2,1,0:T(8,128)S(1)} %slice.2124), channel_id=1, source_target_pairs={{0,1},{1,2},{2,3},{3,4},{4,5},{5,6},{6,7},{8,9},{9,10},{10,11},{11... | collective-permute-start | bytes 98312 | tf_op jit(solution)/shard_map/ppermute | solution.py:12
  218.7 3.1 %collective-permute-start.20 = (f32[2,1,32,128]{3,2,1,0:T(8,128)S(1)}, f32[2,1,32,128]{3,2,1,0:T(8,128)S(1)}, u32[]{:S(2)}, u32[]{:S(2)}) collective-permute-start(f32[2,1,32,128]{3,2,1,0:T(8,128)S(1)} %slice.2138), channel_id=1, source_target_pairs={{1,0},{2,1},{3,2},{4,3},{5,4},{6,5},{7,6},{9,8},{10,9},{11,10},{12... | collective-permute-start | bytes 98312 | tf_op jit(solution)/shard_map/ppermute | solution.py:12
  222.0 6.5 %collective-permute-start.21 = (f32[2,1,32,128]{3,2,1,0:T(8,128)S(1)}, f32[2,1,32,128]{3,2,1,0:T(8,128)S(1)}, u32[]{:S(2)}, u32[]{:S(2)}) collective-permute-start(f32[2,1,32,128]{3,2,1,0:T(8,128)S(1)} %slice.2149), channel_id=1, source_target_pairs={{0,1},{1,2},{2,3},{3,4},{4,5},{5,6},{6,7},{8,9},{9,10},{10,11},{11... | collective-permute-start | bytes 98312 | tf_op jit(solution)/shard_map/ppermute | solution.py:12
  228.8 3.1 %collective-permute-start.22 = (f32[2,1,32,128]{3,2,1,0:T(8,128)S(1)}, f32[2,1,32,128]{3,2,1,0:T(8,128)S(1)}, u32[]{:S(2)}, u32[]{:S(2)}) collective-permute-start(f32[2,1,32,128]{3,2,1,0:T(8,128)S(1)} %slice.2163), channel_id=1, source_target_pairs={{1,0},{2,1},{3,2},{4,3},{5,4},{6,5},{7,6},{9,8},{10,9},{11,10},{12... | collective-permute-start | bytes 98312 | tf_op jit(solution)/shard_map/ppermute | solution.py:12
  232.2 6.5 %collective-permute-start.23 = (f32[2,1,32,128]{3,2,1,0:T(8,128)S(1)}, f32[2,1,32,128]{3,2,1,0:T(8,128)S(1)}, u32[]{:S(2)}, u32[]{:S(2)}) collective-permute-start(f32[2,1,32,128]{3,2,1,0:T(8,128)S(1)} %slice.2174), channel_id=1, source_target_pairs={{0,1},{1,2},{2,3},{3,4},{4,5},{5,6},{6,7},{8,9},{9,10},{10,11},{11... | collective-permute-start | bytes 98312 | tf_op jit(solution)/shard_map/ppermute | solution.py:12
  (35 other events, 33.8 us)
Sparse Core Ops, SparseCore 0:
  240.8 38.4 all-reduce.99
where the time goes:
time: 290 us; the launch traced here: 288 us
  other arithmetic  91.1 us (31%)
  starting transfers between devices  81.2 us (28%)
  waiting for transfers between devices  62.3 us (21%)
  local copies, waits for them, and re-layouts  37.8 us (13%)
  between operations  16 us (6%)
    ppermute x24, starting transfers between devices, from_behind(): return lax.ppermute(block, axis, route)  70 us
    scatter-add x6, other arithmetic, per_device(): source = jnp.zeros((width, depth, span), jnp.float32).at[rec_x, rec_z, re...  49.9 us
    psum x1, waiting for transfers between devices, per_device(): corr_eps, corr_sigma = lax.psum((corr_eps, corr_sigma), 'shot')  38.6 us
    scatter-add x6, other arithmetic, per_device(): source = jnp.zeros((width, depth, span), jnp.float32).at[src_x, src_z, sr...  26.9 us
    ppermute x24, waiting for transfers between devices, from_behind(): return lax.ppermute(block, axis, route)  20.8 us
    gather x6, local copies, waits for them, and re-layouts, per_device(): synth.append(state[0][1][rec_x, rec_z, rec_y])  10.6 us
    unnamed x80, local copies, waits for them, and re-layouts  10.5 us
    all_to_all x1, starting transfers between devices, per_device(): lax.all_to_all(send_pos, 'sub', split_axis=1, concat_axis=1, tiled=True)  7.05 us
  transfers between devices with their start and end apart: 27, of which 18 were waited for; matrix products, arithmetic and copies ran while one was open for 33% of the time, Pallas kernels for 0%

commit v1 on v0

--- a/solution.py
+++ b/solution.py
@@ -113,7 +113,12 @@
     send_trace = jnp.zeros((steps, nsub * CAP), jnp.float32).at[:, target].set(traces)
     send_pos = jnp.full((1, nsub * CAP), -1, jnp.int32).at[0, target].set(cellpos)
     got_trace, got_pos = (
-        lax.all_to_all(send_trace, "sub", split_axis=1, concat_axis=1, tiled=True),
+        jnp.concatenate(
+            lax.all_to_all(
+                jnp.stack(jnp.split(send_trace, lax.axis_size("sub"), axis=1)), "sub", 0, 0
+            ),
+            axis=1,
+        ),
         lax.all_to_all(send_pos, "sub", split_axis=1, concat_axis=1, tiled=True),
     )
     positions = got_pos[0]

time: 290 us -> 294 us (1.014)
  local copies, waits for them, and re-layouts: 37.8 us -> 42.4 us
    unnamed x80 -> x87, local copies, waits for them, and re-layouts: 10.5 us -> 14.6 us
  transfers between devices with their start and end apart: 27 -> 27, of which waited for: 18 -> 18; matrix products, arithmetic and copies ran while one was open for 33% -> 34% of each run, Pallas kernels for 0% -> 0%
where the time goes in v1:
time: 294 us; the launch traced here: 293 us
  other arithmetic  91.1 us (31%)
  starting transfers between devices  81.1 us (28%)
  waiting for transfers between devices  62.3 us (21%)
  local copies, waits for them, and re-layouts  42.4 us (14%)
  between operations  16 us (5%)
    ppermute x24, starting transfers between devices, from_behind(): return lax.ppermute(block, axis, route)  69.9 us
    scatter-add x6, other arithmetic, per_device(): source = jnp.zeros((width, depth, span), jnp.float32).at[rec_x, rec_z, re...  49.9 us
    psum x1, waiting for transfers between devices, per_device(): corr_eps, corr_sigma = lax.psum((corr_eps, corr_sigma), 'shot')  38.6 us
    scatter-add x6, other arithmetic, per_device(): source = jnp.zeros((width, depth, span), jnp.float32).at[src_x, src_z, sr...  26.9 us
    ppermute x24, waiting for transfers between devices, from_behind(): return lax.ppermute(block, axis, route)  20.8 us
    unnamed x87, local copies, waits for them, and re-layouts  14.6 us
    gather x6, local copies, waits for them, and re-layouts, per_device(): synth.append(state[0][1][rec_x, rec_z, rec_y])  10.6 us
    all_to_all x1, starting transfers between devices, per_device(): lax.all_to_all(send_pos, 'sub', split_axis=1, concat_axis=1, tiled=True)  7.05 us
  transfers between devices with their start and end apart: 27, of which 18 were waited for; matrix products, arithmetic and copies ran while one was open for 34% of the time, Pallas kernels for 0%

profile of v1, /device:TPU:0, one launch (start us, length us, event | category | flops | bytes accessed | tf_op | source)
XLA Modules:
  0.0 292.9 jit_solution(10729337079450704631)
XLA Ops:
  13.6 7.1 %all-to-all-start = ((s32[1,8,16]{2,0,1:T(1,128)}), s32[1,8,16]{2,0,1:T(1,128)S(1)}, u32[]{:S(2)}, u32[]{:S(2)}) async-start(s32[1,8,16]{2,0,1:T(1,128)} %bitcast.28), calls=%async_computation | async-start | bytes 8192 | tf_op jit(solution)/shard_map/all_to_all | solution.py:122
  28.5 3.1 %broadcast_multiply_fusion.1 = (f32[64]{0:T(128)S(1)}, f32[64]{0:T(128)S(1)}, f32[64]{0:T(128)S(1)}, f32[64]{0:T(128)S(1)}, f32[64]{0:T(128)S(1)}) fusion(f32[64]{0:T(128)S(1)} %get-tuple-element.205, f32[]{:T(128)} %bitcast.150, f32[]{:T(128)} %bitcast.127, f32[]{:T(128)} %bitcast.104, f32[]{:T(128)} %bitcast.81, f32[]{:T(128)} %bitcast.57), kind=kLoop, calls=%fused_computation.548 | loop fusion | flops 320 | bytes 1556 | tf_op jit(solution)/shard_map/mul | solution.py:137
  31.6 4.5 %scatter_fusion = f32[4,32,128]{2,1,0:T(8,128)S(1)} fusion(f32[4,32,128]{2,1,0:T(8,128)S(1)} %broadcast.880.clone, s32[64]{0:T(128)S(1)} %fusion.152, f32[64]{0:T(128)S(1)} %get-tuple-element.448), kind=kCustom, calls=%fused_computation.7 | custom fusion | flops 64 | bytes 1536 | tf_op jit(solution)/shard_map/scatter-add | solution.py:137
  36.1 4.5 %scatter_fusion.1 = f32[4,32,128]{2,1,0:T(8,128)S(1)} fusion(f32[4,32,128]{2,1,0:T(8,128)S(1)} %broadcast.880.clone.1, s32[64]{0:T(128)S(1)} %fusion.152, f32[64]{0:T(128)S(1)} %get-tuple-element.447), kind=kCustom, calls=%fused_computation.8 | custom fusion | flops 64 | bytes 1536 | tf_op jit(solution)/shard_map/scatter-add | solution.py:137
  40.6 4.5 %scatter_fusion.2 = f32[4,32,128]{2,1,0:T(8,128)S(1)} fusion(f32[4,32,128]{2,1,0:T(8,128)S(1)} %broadcast.880.clone.2, s32[64]{0:T(128)S(1)} %fusion.152, f32[64]{0:T(128)S(1)} %get-tuple-element.446), kind=kCustom, calls=%fused_computation.9 | custom fusion | flops 64 | bytes 1536 | tf_op jit(solution)/shard_map/scatter-add | solution.py:137
  49.3 4.5 %scatter_fusion.3 = f32[4,32,128]{2,1,0:T(8,128)S(1)} fusion(f32[4,32,128]{2,1,0:T(8,128)S(1)} %broadcast.880.clone.3, s32[64]{0:T(128)S(1)} %fusion.152, f32[64]{0:T(128)S(1)} %get-tuple-element.445), kind=kCustom, calls=%fused_computation.10 | custom fusion | flops 64 | bytes 1536 | tf_op jit(solution)/shard_map/scatter-add | solution.py:137
  53.8 4.5 %scatter_fusion.4 = f32[4,32,128]{2,1,0:T(8,128)S(1)} fusion(f32[4,32,128]{2,1,0:T(8,128)S(1)} %broadcast.880.clone.4, s32[64]{0:T(128)S(1)} %fusion.152, f32[64]{0:T(128)S(1)} %get-tuple-element.444), kind=kCustom, calls=%fused_computation.11 | custom fusion | flops 64 | bytes 1536 | tf_op jit(solution)/shard_map/scatter-add | solution.py:137
  58.3 4.5 %scatter_fusion.5 = f32[4,32,128]{2,1,0:T(8,128)S(1)} fusion(f32[4,32,128]{2,1,0:T(8,128)S(1)} %broadcast.880.clone.6, s32[64]{0:T(128)S(1)} %fusion.152, f32[64]{0:T(128)S(1)} %get-tuple-element.204), kind=kCustom, calls=%fused_computation.12 | custom fusion | flops 64 | bytes 1536 | tf_op jit(solution)/shard_map/scatter-add | solution.py:137
  62.8 4.1 %all-to-all-start.1 = ((f32[8,6,16]{2,1,0:T(8,128)}), f32[8,6,16]{2,1,0:T(8,128)S(1)}, u32[]{:S(2)}, u32[]{:S(2)}) async-start(f32[8,6,16]{2,1,0:T(8,128)} %constant_dynamic-update-slice_fusion), calls=%async_computation.1 | async-start | bytes 65536 | tf_op jit(solution)/shard_map/all_to_all | solution.py:117
  68.9 2.8 all-to-all-done.1
  76.2 2.9 collective-permute-start.1
  84.1 3.4 %collective-permute-start.5 = (f32[2,1,32,128]{3,2,1,0:T(8,128)S(1)}, f32[2,1,32,128]{3,2,1,0:T(8,128)S(1)}, u32[]{:S(2)}, u32[]{:S(2)}) collective-permute-start(f32[2,1,32,128]{3,2,1,0:T(8,128)S(1)} %slice.1953), channel_id=1, source_target_pairs={{0,1},{1,2},{2,3},{3,4},{4,5},{5,6},{6,7},{8,9},{9,10},{10,11},{11... | collective-permute-start | bytes 98312 | tf_op jit(solution)/shard_map/ppermute | solution.py:12
  92.4 5.1 %collective-permute-start.7 = (f32[2,1,32,128]{3,2,1,0:T(8,128)S(1)}, f32[2,1,32,128]{3,2,1,0:T(8,128)S(1)}, u32[]{:S(2)}, u32[]{:S(2)}) collective-permute-start(f32[2,1,32,128]{3,2,1,0:T(8,128)S(1)} %slice.1977), channel_id=1, source_target_pairs={{0,1},{1,2},{2,3},{3,4},{4,5},{5,6},{6,7},{8,9},{9,10},{10,11},{11... | collective-permute-start | bytes 98312 | tf_op jit(solution)/shard_map/ppermute | solution.py:12
  100.3 2.0 gather_fusion.2
  103.2 5.0 %collective-permute-start.9 = (f32[2,1,32,128]{3,2,1,0:T(8,128)S(1)}, f32[2,1,32,128]{3,2,1,0:T(8,128)S(1)}, u32[]{:S(2)}, u32[]{:S(2)}) collective-permute-start(f32[2,1,32,128]{3,2,1,0:T(8,128)S(1)} %slice.2001), channel_id=1, source_target_pairs={{0,1},{1,2},{2,3},{3,4},{4,5},{5,6},{6,7},{8,9},{9,10},{10,11},{11... | collective-permute-start | bytes 98312 | tf_op jit(solution)/shard_map/ppermute | solution.py:12
  112.6 2.1 gather_fusion.3
  116.6 3.6 %collective-permute-start.11 = (f32[2,1,32,128]{3,2,1,0:T(8,128)S(1)}, f32[2,1,32,128]{3,2,1,0:T(8,128)S(1)}, u32[]{:S(2)}, u32[]{:S(2)}) collective-permute-start(f32[2,1,32,128]{3,2,1,0:T(8,128)S(1)} %slice.2025), channel_id=1, source_target_pairs={{0,1},{1,2},{2,3},{3,4},{4,5},{5,6},{6,7},{8,9},{9,10},{10,11},{11... | collective-permute-start | bytes 98312 | tf_op jit(solution)/shard_map/ppermute | solution.py:12
  130.6 5.1 %collective-permute-start.13 = (f32[2,1,32,128]{3,2,1,0:T(8,128)S(1)}, f32[2,1,32,128]{3,2,1,0:T(8,128)S(1)}, u32[]{:S(2)}, u32[]{:S(2)}) collective-permute-start(f32[2,1,32,128]{3,2,1,0:T(8,128)S(1)} %slice.2049), channel_id=1, source_target_pairs={{0,1},{1,2},{2,3},{3,4},{4,5},{5,6},{6,7},{8,9},{9,10},{10,11},{11... | collective-permute-start | bytes 98312 | tf_op jit(solution)/shard_map/ppermute | solution.py:12
  140.5 8.3 %scatter_fusion.6 = f32[4,32,128]{2,1,0:T(8,128)S(1)} fusion(f32[4,32,128]{2,1,0:T(8,128)S(1)} %broadcast.880.clone.5, s32[128]{0:T(128)S(1)} %get-tuple-element.216, f32[128]{0:T(128)S(1)} %get-tuple-element.185), kind=kCustom, calls=%fused_computation.14 | custom fusion | flops 128 | bytes 3072 | tf_op jit(solution)/shard_map/scatter-add | solution.py:151
  150.4 8.3 %scatter_fusion.7 = f32[4,32,128]{2,1,0:T(8,128)S(1)} fusion(f32[4,32,128]{2,1,0:T(8,128)S(1)} %broadcast.880.clone.7, s32[128]{0:T(128)S(1)} %get-tuple-element.216, f32[128]{0:T(128)S(1)} %get-tuple-element.184), kind=kCustom, calls=%fused_computation.15 | custom fusion | flops 128 | bytes 3072 | tf_op jit(solution)/shard_map/scatter-add | solution.py:151
  158.8 8.3 %scatter_fusion.8 = f32[4,32,128]{2,1,0:T(8,128)S(1)} fusion(f32[4,32,128]{2,1,0:T(8,128)S(1)} %broadcast.880.clone.8, s32[128]{0:T(128)S(1)} %get-tuple-element.216, f32[128]{0:T(128)S(1)} %get-tuple-element.183), kind=kCustom, calls=%fused_computation.16 | custom fusion | flops 128 | bytes 3072 | tf_op jit(solution)/shard_map/scatter-add | solution.py:151
  167.1 8.3 %scatter_fusion.9 = f32[4,32,128]{2,1,0:T(8,128)S(1)} fusion(f32[4,32,128]{2,1,0:T(8,128)S(1)} %broadcast.880.clone.9, s32[128]{0:T(128)S(1)} %get-tuple-element.216, f32[128]{0:T(128)S(1)} %get-tuple-element.182), kind=kCustom, calls=%fused_computation.17 | custom fusion | flops 128 | bytes 3072 | tf_op jit(solution)/shard_map/scatter-add | solution.py:151
  175.5 8.3 %scatter_fusion.10 = f32[4,32,128]{2,1,0:T(8,128)S(1)} fusion(f32[4,32,128]{2,1,0:T(8,128)S(1)} %broadcast.880.clone.10, s32[128]{0:T(128)S(1)} %get-tuple-element.216, f32[128]{0:T(128)S(1)} %get-tuple-element.181), kind=kCustom, calls=%fused_computation.18 | custom fusion | flops 128 | bytes 3072 | tf_op jit(solution)/shard_map/scatter-add | solution.py:151
  183.8 8.3 %scatter_fusion.11 = f32[4,32,128]{2,1,0:T(8,128)S(1)} fusion(f32[4,32,128]{2,1,0:T(8,128)S(1)} %broadcast.880.clone.11, s32[128]{0:T(128)S(1)} %get-tuple-element.216, f32[128]{0:T(128)S(1)} %get-tuple-element.180), kind=kCustom, calls=%fused_computation.19 | custom fusion | flops 128 | bytes 3072 | tf_op jit(solution)/shard_map/scatter-add | solution.py:151
  192.3 4.4 %collective-permute-start.15 = (f32[2,1,32,128]{3,2,1,0:T(8,128)S(1)}, f32[2,1,32,128]{3,2,1,0:T(8,128)S(1)}, u32[]{:S(2)}, u32[]{:S(2)}) collective-permute-start(f32[2,1,32,128]{3,2,1,0:T(8,128)S(1)} %slice.2074), channel_id=1, source_target_pairs={{0,1},{1,2},{2,3},{3,4},{4,5},{5,6},{6,7},{8,9},{9,10},{10,11},{11... | collective-permute-start | bytes 98312 | tf_op jit(solution)/shard_map/ppermute | solution.py:12
  199.3 4.5 %collective-permute-done.16 = f32[2,1,32,128]{3,2,1,0:T(8,128)S(1)} collective-permute-done((f32[2,1,32,128]{3,2,1,0:T(8,128)S(1)}, f32[2,1,32,128]{3,2,1,0:T(8,128)S(1)}, u32[]{:S(2)}, u32[]{:S(2)}) %collective-permute-start.16) | collective-permute-done | bytes 32800 | tf_op jit(solution)/shard_map/ppermute | solution.py:12
  204.0 5.1 %collective-permute-start.17 = (f32[2,1,32,128]{3,2,1,0:T(8,128)S(1)}, f32[2,1,32,128]{3,2,1,0:T(8,128)S(1)}, u32[]{:S(2)}, u32[]{:S(2)}) collective-permute-start(f32[2,1,32,128]{3,2,1,0:T(8,128)S(1)} %slice.2099), channel_id=1, source_target_pairs={{0,1},{1,2},{2,3},{3,4},{4,5},{5,6},{6,7},{8,9},{9,10},{10,11},{11... | collective-permute-start | bytes 98312 | tf_op jit(solution)/shard_map/ppermute | solution.py:12
  211.8 3.3 %collective-permute-done.18 = f32[2,1,32,128]{3,2,1,0:T(8,128)S(1)} collective-permute-done((f32[2,1,32,128]{3,2,1,0:T(8,128)S(1)}, f32[2,1,32,128]{3,2,1,0:T(8,128)S(1)}, u32[]{:S(2)}, u32[]{:S(2)}) %collective-permute-start.18) | collective-permute-done | bytes 32800 | tf_op jit(solution)/shard_map/ppermute | solution.py:12
  215.3 6.7 %collective-permute-start.19 = (f32[2,1,32,128]{3,2,1,0:T(8,128)S(1)}, f32[2,1,32,128]{3,2,1,0:T(8,128)S(1)}, u32[]{:S(2)}, u32[]{:S(2)}) collective-permute-start(f32[2,1,32,128]{3,2,1,0:T(8,128)S(1)} %slice.2124), channel_id=1, source_target_pairs={{0,1},{1,2},{2,3},{3,4},{4,5},{5,6},{6,7},{8,9},{9,10},{10,11},{11... | collective-permute-start | bytes 98312 | tf_op jit(solution)/shard_map/ppermute | solution.py:12
  226.5 5.7 %collective-permute-start.21 = (f32[2,1,32,128]{3,2,1,0:T(8,128)S(1)}, f32[2,1,32,128]{3,2,1,0:T(8,128)S(1)}, u32[]{:S(2)}, u32[]{:S(2)}) collective-permute-start(f32[2,1,32,128]{3,2,1,0:T(8,128)S(1)} %slice.2149), channel_id=1, source_target_pairs={{0,1},{1,2},{2,3},{3,4},{4,5},{5,6},{6,7},{8,9},{9,10},{10,11},{11... | collective-permute-start | bytes 98312 | tf_op jit(solution)/shard_map/ppermute | solution.py:12
  236.7 5.7 %collective-permute-start.23 = (f32[2,1,32,128]{3,2,1,0:T(8,128)S(1)}, f32[2,1,32,128]{3,2,1,0:T(8,128)S(1)}, u32[]{:S(2)}, u32[]{:S(2)}) collective-permute-start(f32[2,1,32,128]{3,2,1,0:T(8,128)S(1)} %slice.2174), channel_id=1, source_target_pairs={{0,1},{1,2},{2,3},{3,4},{4,5},{5,6},{6,7},{8,9},{9,10},{10,11},{11... | collective-permute-start | bytes 98312 | tf_op jit(solution)/shard_map/ppermute | solution.py:12
  245.2 38.6 %all-reduce.100.cloned.1.call-done = (f32[4,32,128]{2,1,0:T(8,128)}, f32[4,32,128]{2,1,0:T(8,128)}) async-done(((f32[4,32,128]{2,1,0:T(8,128)}, f32[4,32,128]{2,1,0:T(8,128)}), (f32[4,32,128]{2,1,0:T(8,128)}, f32[4,32,128]{2,1,0:T(8,128)})) %all-reduce.100.cloned.1.call-update) | async-done | bytes 131088 | tf_op jit(solution)/shard_map/psum | solution.py:159
  (394 shorter events, 79.8 us)
Async XLA Ops:
  7.2 4.2 %copy-start.31 = (s32[1,128,1]{1,2,0:T(1,128)S(1)}, s32[1,128,1]{1,2,0:T(1,128)}, u32[]{:S(2)}) copy-start(s32[1,128,1]{1,2,0:T(1,128)} %param.55) | copy-start | bytes 1540
  7.2 13.5 %copy-start.2 = (f32[1,3,4,32,128]{4,3,2,1,0:T(8,128)S(1)}, f32[1,3,4,32,128]{4,3,2,1,0:T(8,128)}, u32[]{:S(2)}) copy-start(f32[1,3,4,32,128]{4,3,2,1,0:T(8,128)} %param.41) | copy-start | bytes 589828
  8.0 64.5 %collective-permute-start.2 = (f32[2,1,32,128]{3,2,1,0:T(8,128)S(1)}, f32[2,1,32,128]{3,2,1,0:T(8,128)S(1)}, u32[]{:S(2)}, u32[]{:S(2)}) collective-permute-start(f32[2,1,32,128]{3,2,1,0:T(8,128)S(1)} %slice.1919), channel_id=1, source_target_pairs={{1,0},{2,1},{3,2},{4,3},{5,4},{6,5},{7,6},{9,8},{10,9},{11,10},{12... | collective-permute-start | bytes 98312 | tf_op jit(solution)/shard_map/ppermute | solution.py:12
  10.1 65.1 %collective-permute-start = (f32[2,1,32,128]{3,2,1,0:T(8,128)S(1)}, f32[2,1,32,128]{3,2,1,0:T(8,128)S(1)}, u32[]{:S(2)}, u32[]{:S(2)}) collective-permute-start(f32[2,1,32,128]{3,2,1,0:T(8,128)S(1)} %slice.1899), channel_id=1, source_target_pairs={{1,0},{2,1},{3,2},{4,3},{5,4},{6,5},{7,6},{9,8},{10,9},{11,10},{12... | collective-permute-start | bytes 98312 | tf_op jit(solution)/shard_map/ppermute | solution.py:12
  13.6 49.2 %all-to-all-start = ((s32[1,8,16]{2,0,1:T(1,128)}), s32[1,8,16]{2,0,1:T(1,128)S(1)}, u32[]{:S(2)}, u32[]{:S(2)}) async-start(s32[1,8,16]{2,0,1:T(1,128)} %bitcast.28), calls=%async_computation | async-start | bytes 8192 | tf_op jit(solution)/shard_map/all_to_all | solution.py:122
  26.2 2.1 copy-start.25
  62.8 8.9 %all-to-all-start.1 = ((f32[8,6,16]{2,1,0:T(8,128)}), f32[8,6,16]{2,1,0:T(8,128)S(1)}, u32[]{:S(2)}, u32[]{:S(2)}) async-start(f32[8,6,16]{2,1,0:T(8,128)} %constant_dynamic-update-slice_fusion), calls=%async_computation.1 | async-start | bytes 65536 | tf_op jit(solution)/shard_map/all_to_all | solution.py:117
  66.9 217.0 %all-reduce.100.cloned.1.call-start = ((), (), s32[]{:S(2)}) async-start(), calls=%async_computation.2 | async-start | bytes 262144 | tf_op jit(solution)/shard_map/psum | solution.py:159
  73.5 5.5 %collective-permute-start.3 = (f32[2,1,32,128]{3,2,1,0:T(8,128)S(1)}, f32[2,1,32,128]{3,2,1,0:T(8,128)S(1)}, u32[]{:S(2)}, u32[]{:S(2)}) collective-permute-start(f32[2,1,32,128]{3,2,1,0:T(8,128)S(1)} %slice.1929), channel_id=1, source_target_pairs={{0,1},{1,2},{2,3},{3,4},{4,5},{5,6},{6,7},{8,9},{9,10},{10,11},{11... | collective-permute-start | bytes 98312 | tf_op jit(solution)/shard_map/ppermute | solution.py:12
  76.2 5.2 %collective-permute-start.1 = (f32[2,1,32,128]{3,2,1,0:T(8,128)S(1)}, f32[2,1,32,128]{3,2,1,0:T(8,128)S(1)}, u32[]{:S(2)}, u32[]{:S(2)}) collective-permute-start(f32[2,1,32,128]{3,2,1,0:T(8,128)S(1)} %slice.1909), channel_id=1, source_target_pairs={{0,1},{1,2},{2,3},{3,4},{4,5},{5,6},{6,7},{8,9},{9,10},{10,11},{11... | collective-permute-start | bytes 98312 | tf_op jit(solution)/shard_map/ppermute | solution.py:12
  80.1 3.8 %collective-permute-start.4 = (f32[2,1,32,128]{3,2,1,0:T(8,128)S(1)}, f32[2,1,32,128]{3,2,1,0:T(8,128)S(1)}, u32[]{:S(2)}, u32[]{:S(2)}) collective-permute-start(f32[2,1,32,128]{3,2,1,0:T(8,128)S(1)} %slice.1942), channel_id=1, source_target_pairs={{1,0},{2,1},{3,2},{4,3},{5,4},{6,5},{7,6},{9,8},{10,9},{11,10},{12... | collective-permute-start | bytes 98312 | tf_op jit(solution)/shard_map/ppermute | solution.py:12
  84.1 4.2 %collective-permute-start.5 = (f32[2,1,32,128]{3,2,1,0:T(8,128)S(1)}, f32[2,1,32,128]{3,2,1,0:T(8,128)S(1)}, u32[]{:S(2)}, u32[]{:S(2)}) collective-permute-start(f32[2,1,32,128]{3,2,1,0:T(8,128)S(1)} %slice.1953), channel_id=1, source_target_pairs={{0,1},{1,2},{2,3},{3,4},{4,5},{5,6},{6,7},{8,9},{9,10},{10,11},{11... | collective-permute-start | bytes 98312 | tf_op jit(solution)/shard_map/ppermute | solution.py:12
  88.6 3.7 %collective-permute-start.6 = (f32[2,1,32,128]{3,2,1,0:T(8,128)S(1)}, f32[2,1,32,128]{3,2,1,0:T(8,128)S(1)}, u32[]{:S(2)}, u32[]{:S(2)}) collective-permute-start(f32[2,1,32,128]{3,2,1,0:T(8,128)S(1)} %slice.1966), channel_id=1, source_target_pairs={{1,0},{2,1},{3,2},{4,3},{5,4},{6,5},{7,6},{9,8},{10,9},{11,10},{12... | collective-permute-start | bytes 98312 | tf_op jit(solution)/shard_map/ppermute | solution.py:12
  92.4 6.0 %collective-permute-start.7 = (f32[2,1,32,128]{3,2,1,0:T(8,128)S(1)}, f32[2,1,32,128]{3,2,1,0:T(8,128)S(1)}, u32[]{:S(2)}, u32[]{:S(2)}) collective-permute-start(f32[2,1,32,128]{3,2,1,0:T(8,128)S(1)} %slice.1977), channel_id=1, source_target_pairs={{0,1},{1,2},{2,3},{3,4},{4,5},{5,6},{6,7},{8,9},{9,10},{10,11},{11... | collective-permute-start | bytes 98312 | tf_op jit(solution)/shard_map/ppermute | solution.py:12
  98.7 3.7 %collective-permute-start.8 = (f32[2,1,32,128]{3,2,1,0:T(8,128)S(1)}, f32[2,1,32,128]{3,2,1,0:T(8,128)S(1)}, u32[]{:S(2)}, u32[]{:S(2)}) collective-permute-start(f32[2,1,32,128]{3,2,1,0:T(8,128)S(1)} %slice.1990), channel_id=1, source_target_pairs={{1,0},{2,1},{3,2},{4,3},{5,4},{6,5},{7,6},{9,8},{10,9},{11,10},{12... | collective-permute-start | bytes 98312 | tf_op jit(solution)/shard_map/ppermute | solution.py:12
  103.2 5.9 %collective-permute-start.9 = (f32[2,1,32,128]{3,2,1,0:T(8,128)S(1)}, f32[2,1,32,128]{3,2,1,0:T(8,128)S(1)}, u32[]{:S(2)}, u32[]{:S(2)}) collective-permute-start(f32[2,1,32,128]{3,2,1,0:T(8,128)S(1)} %slice.2001), channel_id=1, source_target_pairs={{0,1},{1,2},{2,3},{3,4},{4,5},{5,6},{6,7},{8,9},{9,10},{10,11},{11... | collective-permute-start | bytes 98312 | tf_op jit(solution)/shard_map/ppermute | solution.py:12
  110.0 4.8 %collective-permute-start.10 = (f32[2,1,32,128]{3,2,1,0:T(8,128)S(1)}, f32[2,1,32,128]{3,2,1,0:T(8,128)S(1)}, u32[]{:S(2)}, u32[]{:S(2)}) collective-permute-start(f32[2,1,32,128]{3,2,1,0:T(8,128)S(1)} %slice.2014), channel_id=1, source_target_pairs={{1,0},{2,1},{3,2},{4,3},{5,4},{6,5},{7,6},{9,8},{10,9},{11,10},{12... | collective-permute-start | bytes 98312 | tf_op jit(solution)/shard_map/ppermute | solution.py:12
  116.6 4.4 %collective-permute-start.11 = (f32[2,1,32,128]{3,2,1,0:T(8,128)S(1)}, f32[2,1,32,128]{3,2,1,0:T(8,128)S(1)}, u32[]{:S(2)}, u32[]{:S(2)}) collective-permute-start(f32[2,1,32,128]{3,2,1,0:T(8,128)S(1)} %slice.2025), channel_id=1, source_target_pairs={{0,1},{1,2},{2,3},{3,4},{4,5},{5,6},{6,7},{8,9},{9,10},{10,11},{11... | collective-permute-start | bytes 98312 | tf_op jit(solution)/shard_map/ppermute | solution.py:12
  123.2 5.6 %collective-permute-start.12 = (f32[2,1,32,128]{3,2,1,0:T(8,128)}, f32[2,1,32,128]{3,2,1,0:T(8,128)}, u32[]{:S(2)}, u32[]{:S(2)}) collective-permute-start(f32[2,1,32,128]{3,2,1,0:T(8,128)} %slice.2038), channel_id=1, source_target_pairs={{1,0},{2,1},{3,2},{4,3},{5,4},{6,5},{7,6},{9,8},{10,9},{11,10},{12... | collective-permute-start | bytes 98312 | tf_op jit(solution)/shard_map/ppermute | solution.py:12
  125.8 2.0 copy-start.20
  127.8 1.7 copy-start.24
  130.6 5.9 %collective-permute-start.13 = (f32[2,1,32,128]{3,2,1,0:T(8,128)S(1)}, f32[2,1,32,128]{3,2,1,0:T(8,128)S(1)}, u32[]{:S(2)}, u32[]{:S(2)}) collective-permute-start(f32[2,1,32,128]{3,2,1,0:T(8,128)S(1)} %slice.2049), channel_id=1, source_target_pairs={{0,1},{1,2},{2,3},{3,4},{4,5},{5,6},{6,7},{8,9},{9,10},{10,11},{11... | collective-permute-start | bytes 98312 | tf_op jit(solution)/shard_map/ppermute | solution.py:12
  148.9 43.2 %collective-permute-start.14 = (f32[2,1,32,128]{3,2,1,0:T(8,128)S(1)}, f32[2,1,32,128]{3,2,1,0:T(8,128)S(1)}, u32[]{:S(2)}, u32[]{:S(2)}) collective-permute-start(f32[2,1,32,128]{3,2,1,0:T(8,128)S(1)} %slice.2063), channel_id=1, source_target_pairs={{1,0},{2,1},{3,2},{4,3},{5,4},{6,5},{7,6},{9,8},{10,9},{11,10},{12... | collective-permute-start | bytes 98312 | tf_op jit(solution)/shard_map/ppermute | solution.py:12
  192.3 5.2 %collective-permute-start.15 = (f32[2,1,32,128]{3,2,1,0:T(8,128)S(1)}, f32[2,1,32,128]{3,2,1,0:T(8,128)S(1)}, u32[]{:S(2)}, u32[]{:S(2)}) collective-permute-start(f32[2,1,32,128]{3,2,1,0:T(8,128)S(1)} %slice.2074), channel_id=1, source_target_pairs={{0,1},{1,2},{2,3},{3,4},{4,5},{5,6},{6,7},{8,9},{9,10},{10,11},{11... | collective-permute-start | bytes 98312 | tf_op jit(solution)/shard_map/ppermute | solution.py:12
  197.8 6.0 %collective-permute-start.16 = (f32[2,1,32,128]{3,2,1,0:T(8,128)S(1)}, f32[2,1,32,128]{3,2,1,0:T(8,128)S(1)}, u32[]{:S(2)}, u32[]{:S(2)}) collective-permute-start(f32[2,1,32,128]{3,2,1,0:T(8,128)S(1)} %slice.2088), channel_id=1, source_target_pairs={{1,0},{2,1},{3,2},{4,3},{5,4},{6,5},{7,6},{9,8},{10,9},{11,10},{12... | collective-permute-start | bytes 98312 | tf_op jit(solution)/shard_map/ppermute | solution.py:12
  204.0 6.0 %collective-permute-start.17 = (f32[2,1,32,128]{3,2,1,0:T(8,128)S(1)}, f32[2,1,32,128]{3,2,1,0:T(8,128)S(1)}, u32[]{:S(2)}, u32[]{:S(2)}) collective-permute-start(f32[2,1,32,128]{3,2,1,0:T(8,128)S(1)} %slice.2099), channel_id=1, source_target_pairs={{0,1},{1,2},{2,3},{3,4},{4,5},{5,6},{6,7},{8,9},{9,10},{10,11},{11... | collective-permute-start | bytes 98312 | tf_op jit(solution)/shard_map/ppermute | solution.py:12
  210.2 4.8 %collective-permute-start.18 = (f32[2,1,32,128]{3,2,1,0:T(8,128)S(1)}, f32[2,1,32,128]{3,2,1,0:T(8,128)S(1)}, u32[]{:S(2)}, u32[]{:S(2)}) collective-permute-start(f32[2,1,32,128]{3,2,1,0:T(8,128)S(1)} %slice.2113), channel_id=1, source_target_pairs={{1,0},{2,1},{3,2},{4,3},{5,4},{6,5},{7,6},{9,8},{10,9},{11,10},{12... | collective-permute-start | bytes 98312 | tf_op jit(solution)/shard_map/ppermute | solution.py:12
  215.3 7.6 %collective-permute-start.19 = (f32[2,1,32,128]{3,2,1,0:T(8,128)S(1)}, f32[2,1,32,128]{3,2,1,0:T(8,128)S(1)}, u32[]{:S(2)}, u32[]{:S(2)}) collective-permute-start(f32[2,1,32,128]{3,2,1,0:T(8,128)S(1)} %slice.2124), channel_id=1, source_target_pairs={{0,1},{1,2},{2,3},{3,4},{4,5},{5,6},{6,7},{8,9},{9,10},{10,11},{11... | collective-permute-start | bytes 98312 | tf_op jit(solution)/shard_map/ppermute | solution.py:12
  223.2 3.1 %collective-permute-start.20 = (f32[2,1,32,128]{3,2,1,0:T(8,128)S(1)}, f32[2,1,32,128]{3,2,1,0:T(8,128)S(1)}, u32[]{:S(2)}, u32[]{:S(2)}) collective-permute-start(f32[2,1,32,128]{3,2,1,0:T(8,128)S(1)} %slice.2138), channel_id=1, source_target_pairs={{1,0},{2,1},{3,2},{4,3},{5,4},{6,5},{7,6},{9,8},{10,9},{11,10},{12... | collective-permute-start | bytes 98312 | tf_op jit(solution)/shard_map/ppermute | solution.py:12
  226.5 6.5 %collective-permute-start.21 = (f32[2,1,32,128]{3,2,1,0:T(8,128)S(1)}, f32[2,1,32,128]{3,2,1,0:T(8,128)S(1)}, u32[]{:S(2)}, u32[]{:S(2)}) collective-permute-start(f32[2,1,32,128]{3,2,1,0:T(8,128)S(1)} %slice.2149), channel_id=1, source_target_pairs={{0,1},{1,2},{2,3},{3,4},{4,5},{5,6},{6,7},{8,9},{9,10},{10,11},{11... | collective-permute-start | bytes 98312 | tf_op jit(solution)/shard_map/ppermute | solution.py:12
  233.4 3.1 %collective-permute-start.22 = (f32[2,1,32,128]{3,2,1,0:T(8,128)S(1)}, f32[2,1,32,128]{3,2,1,0:T(8,128)S(1)}, u32[]{:S(2)}, u32[]{:S(2)}) collective-permute-start(f32[2,1,32,128]{3,2,1,0:T(8,128)S(1)} %slice.2163), channel_id=1, source_target_pairs={{1,0},{2,1},{3,2},{4,3},{5,4},{6,5},{7,6},{9,8},{10,9},{11,10},{12... | collective-permute-start | bytes 98312 | tf_op jit(solution)/shard_map/ppermute | solution.py:12
  236.7 6.5 %collective-permute-start.23 = (f32[2,1,32,128]{3,2,1,0:T(8,128)S(1)}, f32[2,1,32,128]{3,2,1,0:T(8,128)S(1)}, u32[]{:S(2)}, u32[]{:S(2)}) collective-permute-start(f32[2,1,32,128]{3,2,1,0:T(8,128)S(1)} %slice.2174), channel_id=1, source_target_pairs={{0,1},{1,2},{2,3},{3,4},{4,5},{5,6},{6,7},{8,9},{9,10},{10,11},{11... | collective-permute-start | bytes 98312 | tf_op jit(solution)/shard_map/ppermute | solution.py:12
  (35 other events, 34.1 us)
Sparse Core Ops, SparseCore 0:
  245.4 38.4 all-reduce.99
